TPU v7x, 256 devices: a whole 4x4x8 slice. The times are simulated.
256 devices in a mesh: blk: 32 (over x, z_lo, core), uly: 8 (over y, z_hi).
Axes of the slice: x: 4, y: 4, z: 8 (z_hi: 2, z_lo: 4; z = z_hi * 4 + z_lo), core: 2. Of those that a mesh axis runs over, the one named last changes fastest.
Arguments:
- video_tokens: bfloat16 [12288, 3072], P(('blk', 'uly')), may hold values from -6 to 6
- text_tokens: bfloat16 [256, 3072], P('uly'), may hold values from -6 to 6
- video_modulation: bfloat16 [3, 3072], replicated, may hold values from -4 to 4
- text_modulation: bfloat16 [3, 3072], replicated, may hold values from -4 to 4
- video_projection: bfloat16 [3072, 3, 2048], P(None, None, 'uly'), may hold values from -0.109375 to 0.109375
- text_projection: bfloat16 [3072, 3, 2048], P(None, None, 'uly'), may hold values from -0.109375 to 0.109375
- video_output: bfloat16 [2048, 3072], P('uly'), may hold values from -0.125 to 0.125
- text_output: bfloat16 [2048, 3072], P('uly'), may hold values from -0.125 to 0.125
- video_gains: float32 [2, 128], replicated, may hold values from 1 to 12
- text_gains: float32 [2, 128], replicated, may hold values from 1 to 12
Outputs:
- video_attention: bfloat16 [12288, 3072], P(('blk', 'uly'))
- text_attention: bfloat16 [256, 3072], P('uly')
All inputs are finite; a program needn't handle non-finite values.
Results may differ from a plain program's by a relative error of at most 0.025.
The roundings to bfloat16 on the way count: a program that leaves them out, or rounds other values in their place, can miss the bound.
Values may be sent and summed in bfloat16 or wider, within the bound.
A program may use at most 128 MiB of HBM per device.

v0:
```python
import jax
import jax.numpy as jnp
from jax import lax
from jax.sharding import Mesh
from jax.sharding import PartitionSpec as P

HD = 128
BLK = ("blk_0", "blk_1", "blk_2")
ULY = ("uly_0", "uly_1")
BLK_ULY = ("blk_0", "blk_1", "blk_2", "uly_0", "uly_1")
EPS_NORM = 1e-06


def collected_together(x, axis):
    leaves = jax.tree.leaves(x)
    turns = sorted(range(len(leaves)), key=lambda k: -leaves[k].size)
    width = (1, *leaves[turns[0]].shape)[-1]
    lines = [
        jnp.pad(leaves[k].reshape(-1), (0, -leaves[k].size % width)).reshape(-1, width)
        for k in turns
    ]
    both, at, found = (lax.all_gather(jnp.concatenate(lines), axis), 0, {})
    for k, line in zip(turns, lines):
        slab = both[:, at : at + len(line)].reshape(len(both), -1)
        found[k] = slab[:, : leaves[k].size].reshape(-1, *leaves[k].shape)
        at += len(line)
    numbers = iter(range(len(leaves)))
    return jax.tree.map(lambda _: found[next(numbers)], x)


def merged_by_axis(x, axes, combine):
    for axis in axes:
        pieces = collected_together(
            jax.tree.map(
                lambda part, kind: part.astype(kind),
                x,
                jax.tree.map(lambda a: jnp.bfloat16 if a.dtype == jnp.float32 else a.dtype, x),
            ),
            axis,
        )
        widened = [
            jax.tree.map(lambda part, own: part[k].astype(own.dtype), pieces, x)
            for k in range(lax.axis_size(axis))
        ]
        x = widened[0]
        for partner_block in widened[1:]:
            x = combine(x, partner_block)
    return x


def summed_rows(terms, axes):
    subtotal = terms.astype(jnp.bfloat16)
    for axis in axes:
        subtotal = lax.psum_scatter(subtotal, axis, scatter_dimension=0, tiled=True)
    return subtotal.astype(jnp.float32)


def split_up(x, dim, length):
    before, after = (x.shape[:dim], x.shape[dim + 1 :])
    return jnp.moveaxis(x.reshape(*before, length, -1, *after), dim, 0)


def summed_on_arrival(x, axis, dim):
    length = lax.axis_size(axis)
    tiles = lax.all_to_all(split_up(x, dim, length), axis, 0, 0, tiled=True)
    return jnp.sum(tiles.astype(jnp.float32), axis=0)


def modulate(rows, factors):
    floats = rows.astype(jnp.float32)
    centre = floats - jnp.mean(floats, axis=-1, keepdims=True)
    spread = jnp.mean(centre * centre, axis=-1, keepdims=True)
    normed = centre / jnp.sqrt(spread + EPS_NORM)
    wide = factors.astype(jnp.float32)
    return (normed * (1.0 + wide[1]) + wide[0]).astype(jnp.bfloat16)


def head_norm(vectors, channel_gain):
    inverse = lax.rsqrt(jnp.mean(vectors * vectors, axis=-1, keepdims=True) + EPS_NORM)
    return (vectors * inverse * channel_gain).astype(jnp.bfloat16)


def project_rows(modded, weights, gains):
    mixture = jnp.einsum("td,dch->tch", modded, weights, preferred_element_type=jnp.float32)
    row_count, col_count = (mixture.shape[0], mixture.shape[2])
    per_head = mixture.reshape(row_count, 3, col_count // HD, HD)
    query_rows = head_norm(per_head[:, 0], gains[0]).reshape(row_count, col_count)
    key_rows = head_norm(per_head[:, 1], gains[1]).reshape(row_count, col_count)
    value_rows = per_head[:, 2].astype(jnp.bfloat16).reshape(row_count, col_count)
    return jnp.stack([query_rows, key_rows, value_rows], axis=1)


def block_scores(query_rows, key_rows):
    heads_here = query_rows.shape[1] // HD
    return jnp.einsum(
        "qhd,khd->hqk",
        query_rows.reshape(-1, heads_here, HD),
        key_rows.reshape(-1, heads_here, HD),
        preferred_element_type=jnp.float32,
    ) * HD ** (-0.5)


def weighted(weights, value_rows):
    heads_here = weights.shape[0]
    return jnp.einsum(
        "hqk,khd->hqd",
        weights.astype(jnp.bfloat16),
        value_rows.reshape(-1, heads_here, HD),
        preferred_element_type=jnp.float32,
    )


def opening(query_rows, key_rows, value_rows):
    scores = block_scores(query_rows, key_rows)
    highest = jnp.max(scores, axis=-1)
    weights = jnp.exp(scores - highest[..., None])
    return (highest, jnp.sum(weights, axis=-1), weighted(weights, value_rows))


def absorb(softmax_state, query_rows, key_rows, value_rows):
    highest, totals, weighted_sums = softmax_state
    scores = block_scores(query_rows, key_rows)
    raised = jnp.maximum(highest, jnp.max(scores, axis=-1))
    shrink = jnp.exp(highest - raised)
    weights = jnp.exp(scores - raised[..., None])
    return (
        raised,
        totals * shrink + jnp.sum(weights, axis=-1),
        weighted_sums * shrink[..., None] + weighted(weights, value_rows),
    )


def combine_states(earlier_state, later_state):
    raised = jnp.maximum(earlier_state[0], later_state[0])
    left_scale = jnp.exp(earlier_state[0] - raised)
    right_scale = jnp.exp(later_state[0] - raised)
    totals = earlier_state[1] * left_scale + later_state[1] * right_scale
    weighted_sums = (
        earlier_state[2] * left_scale[..., None] + later_state[2] * right_scale[..., None]
    )
    return (raised, totals, weighted_sums)


def finalize(softmax_state):
    result = softmax_state[2] / softmax_state[1][..., None]
    return jnp.transpose(result, (1, 0, 2)).reshape(result.shape[1], -1).astype(jnp.bfloat16)


def joint_attention(softmax_state, query_rows, pairs):
    shard_rows = pairs.shape[0]
    piece_rows = lax.all_gather(pairs, BLK, axis=0, tiled=True)
    turn_count = piece_rows.shape[0] // shard_rows
    turn_rows = piece_rows.shape[0] // turn_count

    def one_turn(turn_index, inner_state):
        sliced = lax.dynamic_slice_in_dim(piece_rows, turn_index * turn_rows, turn_rows, 0)
        return absorb(inner_state, query_rows, sliced[:, 0], sliced[:, 1])

    return lax.fori_loop(0, turn_count, one_turn, softmax_state)


def local(
    video_tokens,
    text_tokens,
    video_modulation,
    text_modulation,
    video_projection,
    text_projection,
    video_output,
    text_output,
    video_gains,
    text_gains,
):
    video_proj = project_rows(
        lax.all_gather(modulate(video_tokens, video_modulation), ULY, axis=0, tiled=True),
        video_projection,
        video_gains,
    )
    text_proj = project_rows(
        lax.all_gather(modulate(text_tokens, text_modulation), ULY, axis=0, tiled=True),
        text_projection,
        text_gains,
    )
    video_pairs = video_proj[:, 1:]
    video_state = opening(video_proj[:, 0], text_proj[:, 1], text_proj[:, 2])
    video_heads = finalize(joint_attention(video_state, video_proj[:, 0], video_pairs))
    text_state = opening(text_proj[:, 0], video_proj[:, 1], video_proj[:, 2])
    text_state = merged_by_axis(text_state, BLK, combine_states)
    text_heads = finalize(absorb(text_state, text_proj[:, 0], text_proj[:, 1], text_proj[:, 2]))
    video_summed = summed_rows(
        jnp.dot(video_heads, video_output, preferred_element_type=jnp.float32), ULY
    )
    text_summed = summed_on_arrival(
        jnp.dot(text_heads, text_output, preferred_element_type=jnp.float32).astype(jnp.bfloat16),
        ULY,
        0,
    )
    video_attention = (video_summed * video_modulation[2].astype(jnp.float32)).astype(jnp.bfloat16)
    text_attention = (text_summed * text_modulation[2].astype(jnp.float32)).astype(jnp.bfloat16)
    return (video_attention, text_attention)


def solution(mesh):
    torus = Mesh(mesh.devices.reshape(4, 4, 2, 4, 2), ("blk_0", "blk_1", "blk_2", "uly_0", "uly_1"))
    placed = (
        P(BLK_ULY, None),
        P(ULY, None),
        P(),
        P(),
        P(None, None, ULY),
        P(None, None, ULY),
        P(ULY, None),
        P(ULY, None),
        P(),
        P(),
    )
    return jax.shard_map(
        local,
        mesh=torus,
        in_specs=placed,
        out_specs=(P(BLK_ULY, None), P(ULY, None)),
        check_vma=False,
    )
```

profile of v0, /device:TPU:32, one launch (start us, length us, event | category | flops | bytes accessed | tf_op | source)
XLA Modules:
  0.0 410.6 jit_solution(2178064178969076653)
XLA Ops:
  8.9 1.1 convert_reduce_fusion.1
  10.0 1.2 fusion.17
  11.2 1.9 fusion.20
  14.6 80.3 %all-gather.7.cloned.1.call-done = bf16[384,3072]{1,0:T(8,128)(2,1)} async-done(((bf16[48,3072]{1,0:T(8,128)(2,1)}), bf16[384,3072]{1,0:T(8,128)(2,1)}) %all-gather.7.cloned.1.call-update) | async-done | bytes 2359312 | tf_op jit(solution)/shard_map/all_gather | solution.py:175
  94.9 5.3 %fusion.5 = f32[384,3,256]{0,2,1:T(8,128)S(1)} fusion(bf16[3072,3,256]{2,0,1:T(8,128)(2,1)} %param.16, bf16[384,3072]{1,0:T(8,128)(2,1)} %all-gather.7.cloned.1.call-done), kind=kOutput, calls=%fused_computation.14 | convolution fusion | flops 1811939328 | bytes 8257536 | tf_op jit(solution)/shard_map/td,dch->tch/dot_general | solution.py:84
  103.9 59.1 %all-gather.9.cloned.1.call-done = bf16[256,3072]{1,0:T(8,128)(2,1)} async-done(((bf16[32,3072]{1,0:T(8,128)(2,1)}), bf16[256,3072]{1,0:T(8,128)(2,1)}) %all-gather.9.cloned.1.call-update) | async-done | bytes 1572880 | tf_op jit(solution)/shard_map/all_gather | solution.py:180
  162.9 5.6 %fusion.7 = f32[256,3,256]{0,2,1:T(8,128)} fusion(bf16[3072,3,256]{2,0,1:T(8,128)(2,1)} %param.17, bf16[256,3072]{1,0:T(8,128)(2,1)} %all-gather.9.cloned.1.call-done), kind=kOutput, calls=%fused_computation.16 | convolution fusion | flops 1207959552 | bytes 7077888 | tf_op jit(solution)/shard_map/td,dch->tch/dot_general | solution.py:84
  171.9 1.2 fusion.156
  175.3 14.7 %all-gather = bf16[2080,128]{1,0:T(8,128)(2,1)S(1)} all-gather(bf16[520,128]{1,0:T(8,128)(2,1)S(1)} %pad_maximum_fusion.1), channel_id=2, replica_groups=mesh['blk_0'=4,'blk_1'=4,'blk_2'=2,'uly_0'=4,'uly_1'=2] {'blk_0'}, dimensions={0}, use_global_device_ids=true | all-gather | bytes 665600 | tf_op jit(solution)/shard_map/all_gather | solution.py:22
  191.7 52.5 %all-gather.11.cloned.1.call-done = bf16[12288,2,256]{0,2,1:T(8,128)(2,1)} async-done(((bf16[384,2,256]{0,2,1:T(8,128)(2,1)}), bf16[12288,2,256]{0,2,1:T(8,128)(2,1)}) %all-gather.11.cloned.1.call-update) | async-done | bytes 12582928 | tf_op jit(solution)/shard_map/all_gather | solution.py:151
  244.2 71.0 %while.17 = (s32[]{:T(128)}, f32[2,384]{1,0:T(2,128)S(1)}, f32[2,384]{1,0:T(2,128)S(1)}, f32[2,384,128]{2,1,0:T(8,128)S(1)}, bf16[12288,2,256]{0,2,1:T(8,128)(2,...) while((s32[]{:T(128)}, f32[2,384]{1,0:T(2,128)S(1)}, ...), condition=%wide.region_12.13_spmd, body=%wide.region_9.12_spmd.sunk | while | flops 152962560 | bytes 5750959 | solution.py:159
  246.4 1.1 constant_dynamic-slice_fusion.3
  248.7 1.1 constant_dynamic-slice_fusion.3
  250.9 1.1 constant_dynamic-slice_fusion.3
  253.1 1.1 constant_dynamic-slice_fusion.3
  255.3 1.1 constant_dynamic-slice_fusion.3
  257.5 1.1 constant_dynamic-slice_fusion.3
  259.8 1.1 constant_dynamic-slice_fusion.3
  262.0 1.1 constant_dynamic-slice_fusion.3
  264.2 1.1 constant_dynamic-slice_fusion.3
  266.4 1.1 constant_dynamic-slice_fusion.3
  268.6 1.1 constant_dynamic-slice_fusion.3
  270.9 1.1 constant_dynamic-slice_fusion.3
  273.1 1.1 constant_dynamic-slice_fusion.3
  315.5 2.2 convolution_convert_fusion
  317.7 15.7 %all-gather.1 = bf16[2080,128]{1,0:T(8,128)(2,1)S(1)} all-gather(bf16[520,128]{1,0:T(8,128)(2,1)S(1)} %pad_maximum_fusion.2), channel_id=3, replica_groups=mesh['blk_0'=4,'blk_1'=4,'blk_2'=2,'uly_0'=4,'uly_1'=2] {'blk_1'}, dimensions={0}, use_global_device_ids=true | all-gather | bytes 665600 | tf_op jit(solution)/shard_map/all_gather | solution.py:22
  334.0 2.0 all-gather.2
  337.8 1.8 convolution_convert_fusion.1
  339.5 6.8 %all-to-all-start = ((bf16[8,32,3072]{2,1,0:T(8,128)(2,1)}), bf16[8,32,3072]{2,1,0:T(8,128)(2,1)S(1)}, u32[]{:S(2)}, u32[]{:S(2)}) async-start(bf16[8,32,3072]{2,1,0:T(8,128)(2,1)} %bitcast.68), calls=%async_computation.2 | async-start | bytes 3145728 | tf_op jit(solution)/shard_map/all_to_all | solution.py:65
  346.4 4.9 %reduce-scatter.3.cloned.1.call-done = bf16[96,3072]{1,0:T(8,128)(2,1)} async-done(((bf16[384,3072]{1,0:T(8,128)(2,1)}), bf16[96,3072]{1,0:T(8,128)(2,1)}) %reduce-scatter.3.cloned.1.call-update) | async-done | bytes 589840 | tf_op jit(solution)/shard_map/reduce_scatter | solution.py:54
  351.4 50.1 %all-to-all-done = bf16[8,32,3072]{2,1,0:T(8,128)(2,1)S(1)} async-done(((bf16[8,32,3072]{2,1,0:T(8,128)(2,1)}), bf16[8,32,3072]{2,1,0:T(8,128)(2,1)S(1)}, u32[]{:S(2)}, u32[]{:S(2)}) %all-to-all-start) | async-done | bytes 1572896 | tf_op jit(solution)/shard_map/all_to_all | solution.py:65
  402.4 1.7 multiply_convert_fusion
  (319 shorter events, 72.7 us)
Async XLA Ops:
  7.2 308.3 %copy-start = (bf16[256,3072]{1,0:T(8,128)(2,1)S(1)}, bf16[256,3072]{1,0:T(8,128)(2,1)}, u32[]{:S(2)}) copy-start(bf16[256,3072]{1,0:T(8,128)(2,1)} %param.18) | copy-start | bytes 4718596
  7.2 6.0 %copy-start.9 = (bf16[3,3072]{1,0:T(4,128)(2,1)S(1)}, bf16[3,3072]{1,0:T(4,128)(2,1)}, u32[]{:S(2)}) copy-start(bf16[3,3072]{1,0:T(4,128)(2,1)} %param.15) | copy-start | bytes 55300
  7.2 6.0 %copy-start.3 = (bf16[32,3072]{1,0:T(8,128)(2,1)S(1)}, bf16[32,3072]{1,0:T(8,128)(2,1)}, u32[]{:S(2)}) copy-start(bf16[32,3072]{1,0:T(8,128)(2,1)} %param.13) | copy-start | bytes 589828
  7.2 7.4 %copy-start.10 = (f32[2,128]{1,0:T(2,128)S(1)}, f32[2,128]{1,0:T(2,128)}, u32[]{:S(2)}) copy-start(f32[2,128]{1,0:T(2,128)} %param.21) | copy-start | bytes 3076
  7.2 7.4 %copy-start.11 = (f32[2,128]{1,0:T(2,128)S(1)}, f32[2,128]{1,0:T(2,128)}, u32[]{:S(2)}) copy-start(f32[2,128]{1,0:T(2,128)} %param.20) | copy-start | bytes 3076
  7.2 87.7 %all-gather.7.cloned.1.call-start = ((), (), s32[]{:S(2)}) async-start(), calls=%async_computation.3 | async-start | bytes 2654208 | tf_op jit(solution)/shard_map/all_gather | solution.py:175
  13.1 149.8 %all-gather.9.cloned.1.call-start = ((), (), s32[]{:S(2)}) async-start(), calls=%async_computation.4 | async-start | bytes 1769472 | tf_op jit(solution)/shard_map/all_gather | solution.py:180
  14.5 229.7 %all-gather.11.cloned.1.call-start = ((), (), s32[]{:S(2)}) async-start(), calls=%async_computation.5 | async-start | bytes 12976128 | tf_op jit(solution)/shard_map/all_gather | solution.py:151
  102.1 0.9 copy-start.6
  103.8 247.5 %reduce-scatter.3.cloned.1.call-start = ((), (), s32[]{:S(2)}) async-start(), calls=%async_computation.6 | async-start | bytes 2949120 | tf_op jit(solution)/shard_map/reduce_scatter | solution.py:54
  171.3 1.8 copy-start.5
  174.9 15.6 %copy-start.1 = (f32[384,1,2,128]{3,0,2,1:T(8,128)S(1)}, f32[384,1,2,128]{3,0,2,1:T(8,128)}, u32[]{:S(2)}) copy-start(f32[384,1,2,128]{3,0,2,1:T(8,128)} %copy.54) | copy-start | bytes 1179652
  190.5 0.9 copy-start.7
  317.7 18.6 %copy-start.2 = (f32[2,256,256]{1,2,0:T(8,128)S(1)}, f32[2,256,256]{1,2,0:T(8,128)}, u32[]{:S(2)}) copy-start(f32[2,256,256]{1,2,0:T(8,128)} %get-tuple-element.171) | copy-start | bytes 1572868
  336.3 1.4 copy-start.4
  339.5 6.9 %copy-start.8 = (bf16[3,3072]{1,0:T(4,128)(2,1)S(1)}, bf16[3,3072]{1,0:T(4,128)(2,1)}, u32[]{:S(2)}) copy-start(bf16[3,3072]{1,0:T(4,128)(2,1)} %param.14) | copy-start | bytes 55300
  339.5 61.9 %all-to-all-start = ((bf16[8,32,3072]{2,1,0:T(8,128)(2,1)}), bf16[8,32,3072]{2,1,0:T(8,128)(2,1)S(1)}, u32[]{:S(2)}, u32[]{:S(2)}) async-start(bf16[8,32,3072]{2,1,0:T(8,128)(2,1)} %bitcast.68), calls=%async_computation.2 | async-start | bytes 3145728 | tf_op jit(solution)/shard_map/all_to_all | solution.py:65
  346.3 56.1 %reduce-scatter.5.cloned.1.call-start = ((), (), s32[]{:S(2)}) async-start(), calls=%async_computation.7 | async-start | bytes 884736 | tf_op jit(solution)/shard_map/reduce_scatter | solution.py:54
Sparse Core Ops, SparseCore 0:
  13.2 81.6 all-gather.6
  98.1 64.7 all-gather.8
  164.7 79.4 all-gather.10
  317.8 33.4 reduce-scatter.2
  353.7 44.8 reduce-scatter.4
where the time goes:
time: 412 us; the launch traced here: 411 us
  waiting for transfers between devices  247 us (60%)
  matrix products  46.4 us (11%)
  local copies, waits for them, and re-layouts  43.2 us (10%)
  blocking collectives  32.4 us (8%)
  other arithmetic  18.7 us (5%)
  between operations  14.3 us (3%)
  starting transfers between devices  7 us (2%)
    all_gather x1, waiting for transfers between devices, local(): lax.all_gather(modulate(video_tokens, video_modulation), ULY, axis=0, til...  80.3 us
    all_gather x1, waiting for transfers between devices, local(): lax.all_gather(modulate(text_tokens, text_modulation), ULY, axis=0, tiled...  59.1 us
    all_gather x1, waiting for transfers between devices, joint_attention(): piece_rows = lax.all_gather(pairs, BLK, axis=0, tiled=True)  52.5 us
    all_to_all x1, waiting for transfers between devices, summed_on_arrival(): tiles = lax.all_to_all(split_up(x, dim, length), axis, 0, 0, tiled=True)  50.1 us
    slice x32, local copies, waits for them, and re-layouts, one_turn(): return absorb(inner_state, query_rows, sliced[:, 0], sliced[:, 1])  34.2 us
    all_gather x3, blocking collectives, collected_together(): both, at, found = (lax.all_gather(jnp.concatenate(lines), axis), 0, {})  32.4 us
    dot_general x35, matrix products, weighted(): jnp.einsum('hqk,khd->hqd', weights.astype(jnp.bfloat16), value_rows.resha...  17.2 us
    dot_general x35, matrix products, block_scores(): jnp.einsum('qhd,khd->hqk', query_rows.reshape(-1, heads_here, HD), key_ro...  14.2 us
  transfers between devices with their start and end apart: 6, of which 5 were waited for; matrix products, arithmetic and copies ran while one was open for 7% of the time, Pallas kernels for 0%

commit v1 on v0

--- a/solution.py
+++ b/solution.py
@@ -3,6 +3,7 @@
 from jax import lax
 from jax.sharding import Mesh
 from jax.sharding import PartitionSpec as P
+from jax.lax import all_to_all, axis_size
 
 HD = 128
 BLK = ("blk_0", "blk_1", "blk_2")
@@ -176,10 +177,15 @@
         video_projection,
         video_gains,
     )
+
+    def pack_body_up(x_local, pos_dim):
+        return jnp.concatenate(
+            all_to_all(jnp.stack([x_local for _ in range(axis_size(ULY))], axis=0), ULY, 0, 0),
+            axis=pos_dim,
+        )
+
     text_proj = project_rows(
-        lax.all_gather(modulate(text_tokens, text_modulation), ULY, axis=0, tiled=True),
-        text_projection,
-        text_gains,
+        pack_body_up(modulate(text_tokens, text_modulation), 0), text_projection, text_gains
     )
     video_pairs = video_proj[:, 1:]
     video_state = opening(video_proj[:, 0], text_proj[:, 1], text_proj[:, 2])

time: 412 us -> 383 us (0.930)
  waiting for transfers between devices: 247 us -> 206 us
  local copies, waits for them, and re-layouts: 43.2 us -> 49.6 us
  starting transfers between devices: 7 us -> 12.9 us
    all_gather x1 -> x0, waiting for transfers between devices: 59.1 us -> none  [local(): lax.all_gather(modulate(text_tokens, text_modulation), ULY, axis=0, tiled...]
    all_to_all x0 -> x1, waiting for transfers between devices: none -> 50 us  [pack_body_up(): all_to_all(jnp.stack([x_local for _ in range(axis_size(ULY))], axis=0), U...]
    all_gather x1, waiting for transfers between devices: 52.5 us -> 20.1 us  [joint_attention(): piece_rows = lax.all_gather(pairs, BLK, axis=0, tiled=True)]
    dot_general x0 -> x1, local copies, waits for them, and re-layouts: none -> 6.83 us  [project_rows(): jnp.einsum('td,dch->tch', modded, weights, preferred_element_type=jnp.flo...]
    all_to_all x0 -> x1, starting transfers between devices: none -> 4.29 us  [pack_body_up(): all_to_all(jnp.stack([x_local for _ in range(axis_size(ULY))], axis=0), U...]
where the time goes in v1:
time: 383 us; the launch traced here: 382 us
  waiting for transfers between devices  206 us (54%)
  local copies, waits for them, and re-layouts  49.6 us (13%)
  matrix products  47.2 us (12%)
  blocking collectives  30.9 us (8%)
  other arithmetic  19.3 us (5%)
  between operations  14.2 us (4%)
  starting transfers between devices  12.9 us (3%)
    all_gather x1, waiting for transfers between devices, local(): lax.all_gather(modulate(video_tokens, video_modulation), ULY, axis=0, til...  80.6 us
    all_to_all x1, waiting for transfers between devices, summed_on_arrival(): tiles = lax.all_to_all(split_up(x, dim, length), axis, 0, 0, tiled=True)  50.5 us
    all_to_all x1, waiting for transfers between devices, pack_body_up(): all_to_all(jnp.stack([x_local for _ in range(axis_size(ULY))], axis=0), U...  50 us
    slice x32, local copies, waits for them, and re-layouts, one_turn(): return absorb(inner_state, query_rows, sliced[:, 0], sliced[:, 1])  34.2 us
    all_gather x3, blocking collectives, collected_together(): both, at, found = (lax.all_gather(jnp.concatenate(lines), axis), 0, {})  30.9 us
    all_gather x1, waiting for transfers between devices, joint_attention(): piece_rows = lax.all_gather(pairs, BLK, axis=0, tiled=True)  20.1 us
    dot_general x35, matrix products, weighted(): jnp.einsum('hqk,khd->hqd', weights.astype(jnp.bfloat16), value_rows.resha...  19.2 us
    dot_general x35, matrix products, block_scores(): jnp.einsum('qhd,khd->hqk', query_rows.reshape(-1, heads_here, HD), key_ro...  14.4 us
  transfers between devices with their start and end apart: 6, of which 5 were waited for; matrix products, arithmetic and copies ran while one was open for 7% of the time, Pallas kernels for 0%

profile of v1, /device:TPU:32, one launch (start us, length us, event | category | flops | bytes accessed | tf_op | source)
XLA Modules:
  0.0 381.6 jit_solution(18282657817665019766)
XLA Ops:
  8.8 1.1 convert_reduce_fusion.1
  10.0 1.2 fusion.15
  11.2 1.9 fusion.18
  14.3 80.6 %all-gather.6.cloned.1.call-done = bf16[384,3072]{1,0:T(8,128)(2,1)} async-done(((bf16[48,3072]{1,0:T(8,128)(2,1)}), bf16[384,3072]{1,0:T(8,128)(2,1)}) %all-gather.6.cloned.1.call-update) | async-done | bytes 2359312 | tf_op jit(solution)/shard_map/all_gather | solution.py:176
  94.9 5.3 %fusion.5 = f32[384,3,256]{0,2,1:T(8,128)S(1)} fusion(bf16[3072,3,256]{2,0,1:T(8,128)(2,1)} %param.16, bf16[384,3072]{1,0:T(8,128)(2,1)} %all-gather.6.cloned.1.call-done), kind=kOutput, calls=%fused_computation.14 | convolution fusion | flops 1811939328 | bytes 8257536 | tf_op jit(solution)/shard_map/td,dch->tch/dot_general | solution.py:85
  104.8 1.3 stack.4
  106.1 4.3 %all-to-all-start = ((bf16[8,32,3072]{2,1,0:T(8,128)(2,1)}), bf16[8,32,3072]{2,1,0:T(8,128)(2,1)}, u32[]{:S(2)}, u32[]{:S(2)}) async-start(bf16[8,32,3072]{2,1,0:T(8,128)(2,1)} %stack.4), calls=%async_computation | async-start | bytes 3145728 | tf_op jit(solution)/shard_map/all_to_all | solution.py:183
  110.5 6.8 %copy.60 = bf16[3,256,3072]{2,1,0:T(8,128)(2,1)} copy(bf16[3,256,3072]{1,2,0:T(8,128)(2,1)} %bitcast.619) | data formatting | bytes 9437184 | tf_op jit(solution)/shard_map/td,dch->tch/dot_general | solution.py:85
  117.3 50.0 %all-to-all-done = bf16[8,32,3072]{2,1,0:T(8,128)(2,1)} async-done(((bf16[8,32,3072]{2,1,0:T(8,128)(2,1)}), bf16[8,32,3072]{2,1,0:T(8,128)(2,1)}, u32[]{:S(2)}, u32[]{:S(2)}) %all-to-all-start) | async-done | bytes 1572896 | tf_op jit(solution)/shard_map/all_to_all | solution.py:183
  167.3 4.3 %fusion.144 = f32[256,3,2,128]{0,3,2,1:T(8,128)S(1)} fusion(bf16[256,3072,1,1]{1,0,3,2:T(8,128)(2,1)} %bitcast.13, bf16[3,2,128,3072]{3,2,1,0:T(8,128)(2,1)} %bitcast.620), kind=kOutput, calls=%fused_computation.247 | convolution fusion | flops 1207959552 | bytes 7077888 | tf_op jit(solution)/shard_map/td,dch->tch/dot_general | solution.py:85
  171.8 1.2 fusion.142
  174.4 1.2 copy.61
  175.6 1.3 convolution_convert_fusion.2
  177.6 14.2 %all-gather = bf16[2080,128]{1,0:T(8,128)(2,1)S(1)} all-gather(bf16[520,128]{1,0:T(8,128)(2,1)S(1)} %pad_maximum_fusion.1), channel_id=2, replica_groups=mesh['blk_0'=4,'blk_1'=4,'blk_2'=2,'uly_0'=4,'uly_1'=2] {'blk_0'}, dimensions={0}, use_global_device_ids=true | all-gather | bytes 665600 | tf_op jit(solution)/shard_map/all_gather | solution.py:23
  193.5 20.1 %all-gather.8.cloned.1.call-done = bf16[12288,2,256]{0,2,1:T(8,128)(2,1)} async-done(((bf16[384,2,256]{0,2,1:T(8,128)(2,1)}), bf16[12288,2,256]{0,2,1:T(8,128)(2,1)}) %all-gather.8.cloned.1.call-update) | async-done | bytes 12582928 | tf_op jit(solution)/shard_map/all_gather | solution.py:152
  213.6 71.0 %while.17 = (s32[]{:T(128)}, f32[2,384]{1,0:T(2,128)S(1)}, f32[2,384]{1,0:T(2,128)S(1)}, f32[2,384,128]{2,1,0:T(8,128)S(1)}, bf16[12288,2,256]{0,2,1:T(8,128)(2,...) while((s32[]{:T(128)}, f32[2,384]{1,0:T(2,128)S(1)}, ...), condition=%wide.region_12.13_spmd, body=%wide.region_9.12_spmd.sunk | while | flops 152962560 | bytes 5750959 | solution.py:160
  215.9 1.1 constant_dynamic-slice_fusion.3
  222.5 1.1 constant_dynamic-slice_fusion.3
  229.2 1.1 constant_dynamic-slice_fusion.3
  233.6 1.1 constant_dynamic-slice_fusion.3
  240.3 1.1 constant_dynamic-slice_fusion.3
  244.7 1.1 constant_dynamic-slice_fusion.3
  251.4 1.1 constant_dynamic-slice_fusion.3
  284.9 2.2 convolution_convert_fusion
  287.2 14.7 %all-gather.1 = bf16[2080,128]{1,0:T(8,128)(2,1)S(1)} all-gather(bf16[520,128]{1,0:T(8,128)(2,1)S(1)} %pad_maximum_fusion.2), channel_id=3, replica_groups=mesh['blk_0'=4,'blk_1'=4,'blk_2'=2,'uly_0'=4,'uly_1'=2] {'blk_1'}, dimensions={0}, use_global_device_ids=true | all-gather | bytes 665600 | tf_op jit(solution)/shard_map/all_gather | solution.py:23
  302.5 2.0 all-gather.2
  305.6 1.3 fusion.8
  307.0 1.8 convolution_convert_fusion.1
  308.8 8.5 %all-to-all-start.1 = ((bf16[8,32,3072]{2,1,0:T(8,128)(2,1)}), bf16[8,32,3072]{2,1,0:T(8,128)(2,1)S(1)}, u32[]{:S(2)}, u32[]{:S(2)}) async-start(bf16[8,32,3072]{2,1,0:T(8,128)(2,1)} %bitcast.71), calls=%async_computation.3 | async-start | bytes 3145728 | tf_op jit(solution)/shard_map/all_to_all | solution.py:66
  317.3 4.6 %reduce-scatter.3.cloned.1.call-done = bf16[96,3072]{1,0:T(8,128)(2,1)} async-done(((bf16[384,3072]{1,0:T(8,128)(2,1)}), bf16[96,3072]{1,0:T(8,128)(2,1)}) %reduce-scatter.3.cloned.1.call-update) | async-done | bytes 589840 | tf_op jit(solution)/shard_map/reduce_scatter | solution.py:55
  321.9 50.5 %all-to-all-done.1 = bf16[8,32,3072]{2,1,0:T(8,128)(2,1)S(1)} async-done(((bf16[8,32,3072]{2,1,0:T(8,128)(2,1)}), bf16[8,32,3072]{2,1,0:T(8,128)(2,1)S(1)}, u32[]{:S(2)}, u32[]{:S(2)}) %all-to-all-start.1) | async-done | bytes 1572896 | tf_op jit(solution)/shard_map/all_to_all | solution.py:66
  373.3 1.7 multiply_convert_fusion
  (320 shorter events, 76.2 us)
Async XLA Ops:
  7.2 277.8 %copy-start = (bf16[256,3072]{1,0:T(8,128)(2,1)S(1)}, bf16[256,3072]{1,0:T(8,128)(2,1)}, u32[]{:S(2)}) copy-start(bf16[256,3072]{1,0:T(8,128)(2,1)} %param.18) | copy-start | bytes 4718596
  7.2 6.0 %copy-start.14 = (f32[2,128]{1,0:T(2,128)S(1)}, f32[2,128]{1,0:T(2,128)}, u32[]{:S(2)}) copy-start(f32[2,128]{1,0:T(2,128)} %param.20) | copy-start | bytes 3076
  7.2 6.0 %copy-start.13 = (f32[2,128]{1,0:T(2,128)S(1)}, f32[2,128]{1,0:T(2,128)}, u32[]{:S(2)}) copy-start(f32[2,128]{1,0:T(2,128)} %param.21) | copy-start | bytes 3076
  7.2 87.7 %all-gather.6.cloned.1.call-start = ((), (), s32[]{:S(2)}) async-start(), calls=%async_computation.4 | async-start | bytes 2654208 | tf_op jit(solution)/shard_map/all_gather | solution.py:176
  13.1 200.5 %all-gather.8.cloned.1.call-start = ((), (), s32[]{:S(2)}) async-start(), calls=%async_computation.5 | async-start | bytes 12976128 | tf_op jit(solution)/shard_map/all_gather | solution.py:152
  13.8 0.6 copy-start.10
  101.6 15.8 %copy-start.3 = (bf16[384,1,2,128]{3,0,2,1:T(8,128)(2,1)}, bf16[384,1,2,128]{3,0,2,1:T(8,128)(2,1)S(1)}, u32[]{:S(2)}) copy-start(bf16[384,1,2,128]{3,0,2,1:T(8,128)(2,1)S(1)} %copy.63) | copy-start | bytes 589828
  101.6 2.6 copy-start.2
  106.1 61.2 %all-to-all-start = ((bf16[8,32,3072]{2,1,0:T(8,128)(2,1)}), bf16[8,32,3072]{2,1,0:T(8,128)(2,1)}, u32[]{:S(2)}, u32[]{:S(2)}) async-start(bf16[8,32,3072]{2,1,0:T(8,128)(2,1)} %stack.4), calls=%async_computation | async-start | bytes 3145728 | tf_op jit(solution)/shard_map/all_to_all | solution.py:183
  110.4 211.5 %reduce-scatter.3.cloned.1.call-start = ((), (), s32[]{:S(2)}) async-start(), calls=%async_computation.6 | async-start | bytes 2949120 | tf_op jit(solution)/shard_map/reduce_scatter | solution.py:55
  167.3 4.4 %copy-start.7 = (f32[128]{0:T(128)S(1)}, f32[128]{0:T(128)}, u32[]{:S(2)}) copy-start(f32[128]{0:T(128)} %get-tuple-element.165) | copy-start | bytes 1540
  167.3 4.4 %copy-start.9 = (f32[128]{0:T(128)S(1)}, f32[128]{0:T(128)}, u32[]{:S(2)}) copy-start(f32[128]{0:T(128)} %get-tuple-element.164) | copy-start | bytes 1540
  171.7 1.3 copy-start.11
  175.6 16.9 %copy-start.12 = (f32[128]{0:T(128)S(1)}, f32[128]{0:T(128)}, u32[]{:S(2)}) copy-start(f32[128]{0:T(128)} %get-tuple-element.176) | copy-start | bytes 1540
  176.8 15.8 %copy-start.8 = (f32[128]{0:T(128)S(1)}, f32[128]{0:T(128)}, u32[]{:S(2)}) copy-start(f32[128]{0:T(128)} %get-tuple-element.165) | copy-start | bytes 1540
  287.2 18.3 %copy-start.1 = (f32[2,256,256]{1,2,0:T(8,128)S(1)}, f32[2,256,256]{1,2,0:T(8,128)}, u32[]{:S(2)}) copy-start(f32[2,256,256]{1,2,0:T(8,128)} %get-tuple-element.171) | copy-start | bytes 1572868
  305.5 1.5 copy-start.4
  308.8 8.5 %copy-start.5 = (bf16[3,3072]{1,0:T(4,128)(2,1)S(1)}, bf16[3,3072]{1,0:T(4,128)(2,1)}, u32[]{:S(2)}) copy-start(bf16[3,3072]{1,0:T(4,128)(2,1)} %param.15) | copy-start | bytes 55300
  308.8 13.1 %copy-start.6 = (bf16[3,3072]{1,0:T(4,128)(2,1)S(1)}, bf16[3,3072]{1,0:T(4,128)(2,1)}, u32[]{:S(2)}) copy-start(bf16[3,3072]{1,0:T(4,128)(2,1)} %param.14) | copy-start | bytes 55300
  308.8 63.6 %all-to-all-start.1 = ((bf16[8,32,3072]{2,1,0:T(8,128)(2,1)}), bf16[8,32,3072]{2,1,0:T(8,128)(2,1)S(1)}, u32[]{:S(2)}, u32[]{:S(2)}) async-start(bf16[8,32,3072]{2,1,0:T(8,128)(2,1)} %bitcast.71), calls=%async_computation.3 | async-start | bytes 3145728 | tf_op jit(solution)/shard_map/all_to_all | solution.py:66
  317.2 56.1 %reduce-scatter.5.cloned.1.call-start = ((), (), s32[]{:S(2)}) async-start(), calls=%async_computation.7 | async-start | bytes 884736 | tf_op jit(solution)/shard_map/reduce_scatter | solution.py:55
Sparse Core Ops, SparseCore 0:
  13.2 81.6 all-gather.5
  102.8 110.7 all-gather.7
  287.3 34.5 reduce-scatter.2
  324.2 45.1 reduce-scatter.4
